TPU v7x, 256 devices: a whole 4x4x8 slice. The times are simulated.
256 devices in a mesh: row: 32 (over y, x, z_hi), col: 8 (over z_lo, core).
Axes of the slice: x: 4, y: 4, z: 8 (z_hi: 2, z_lo: 4; z = z_hi * 4 + z_lo), core: 2. Of those that a mesh axis runs over, the one named last changes fastest.
Arguments:
- hamiltonian_blocks: bfloat16 [32, 8, 64, 128, 128], P('row', 'col'), may hold values from -0.046875 to 0.046875
- block_rows: int32 [32, 8, 64], P('row', 'col'), may hold values from 0 to 7, as said below
- block_cols: int32 [32, 8, 64], P('row', 'col'), may hold values from 0 to 31
- block_counts: int32 [32, 8], P('row', 'col'), may hold values from 16 to 64, as said below
- initial: float32 [32768, 128], P(('row', 'col')), may hold values from -6 to 6
- center: float32 [1], replicated, may hold values from -0.3 to 0.3
- halfwidth: float32 [1], replicated, may hold values from 1 to 1.5
Outputs:
- filtered: float32 [32768, 128], P(('row', 'col'))
Inputs may be any that keep to these rules, and one draw needn't show every extreme that they name: `block_rows`: padded slots hold arbitrary values. `block_counts`: some tile is full in every draw.
All inputs are finite; a program needn't handle non-finite values.
Results may differ from a plain program's by a relative error of at most 0.0068.
Values may be sent and summed in bfloat16 or wider, within the bound.
A program may use at most 128 MiB of HBM per device.

v0:
```python
import jax
import jax.numpy as jnp
from jax import lax
from jax.sharding import PartitionSpec as P

SLAB = 1
DEGREE = 3


def body(hamiltonian_blocks, block_rows, block_cols, block_counts, initial, center, halfwidth):
    stacked = hamiltonian_blocks[0, 0]
    slot_rows = block_rows[0, 0]
    slot_cols = block_cols[0, 0]
    live_count = block_counts[0, 0]
    grid_rows = lax.axis_size("row")
    grid_cols = lax.axis_size("col")
    orbitals = stacked.shape[1]
    vectors = initial.shape[1]
    slots = stacked.shape[0]
    row_segments = grid_cols * SLAB
    col_segments = grid_rows * SLAB
    highest = lax.Precision.HIGHEST
    is_live = jnp.arange(slots, dtype=jnp.int32) < live_count
    row_onehot = (
        (slot_rows[None, :] == jnp.arange(row_segments, dtype=jnp.int32)[:, None])
        & is_live[None, :]
    ).astype(jnp.float32)
    col_onehot = (
        (slot_cols[None, :] == jnp.arange(col_segments, dtype=jnp.int32)[:, None])
        & is_live[None, :]
    ).astype(jnp.float32)
    previous = initial
    current = initial
    for degree_step in range(DEGREE):
        panel = current.astype(jnp.bfloat16)
        apply_column_panel = lax.all_gather(panel, "row", axis=0, tiled=True).reshape(
            -1, orbitals, vectors
        )
        apply_row_panel = lax.all_gather(panel, "col", axis=0, tiled=True).reshape(
            -1, orbitals, vectors
        )
        upper_products = jnp.einsum(
            "sab,sbv->sav",
            stacked,
            apply_column_panel[slot_cols],
            preferred_element_type=jnp.float32,
        )
        upper_partial = jnp.einsum("ts,sav->tav", row_onehot, upper_products, precision=highest)
        upper_sum = lax.psum_scatter(
            upper_partial.reshape(-1, vectors), "col", scatter_dimension=0, tiled=True
        )
        products = jnp.einsum(
            "sba,sbv->sav", stacked, apply_row_panel[slot_rows], preferred_element_type=jnp.float32
        )
        lower_partial = jnp.einsum("ts,sav->tav", col_onehot, products, precision=highest)
        lower_sum = lax.psum_scatter(
            lower_partial.reshape(-1, vectors), "row", scatter_dimension=0, tiled=True
        )
        applied = upper_sum + lower_sum
        shifted = (applied - center[0] * current) / halfwidth[0]
        if degree_step == 0:
            following = shifted
        else:
            following = 2.0 * shifted - previous
        previous = current
        current = following
    return current


def solution(mesh):
    in_specs = (
        P("row", "col", None, None, None),
        P("row", "col", None),
        P("row", "col", None),
        P("row", "col"),
        P(("row", "col"), None),
        P(),
        P(),
    )
    out_specs = P(("row", "col"), None)
    return jax.shard_map(body, mesh=mesh, in_specs=in_specs, out_specs=out_specs, check_vma=False)
```

profile of v0, /device:TPU:32, one launch (start us, length us, event | category | flops | bytes accessed | tf_op | source)
XLA Modules:
  0.0 1112.5 jit_solution(9385953845992300890)
XLA Ops:
  9.6 83.8 %all-gather.4.cloned.1.call-done = bf16[4096,128]{1,0:T(8,128)(2,1)} async-done(((bf16[128,128]{1,0:T(8,128)(2,1)}), bf16[4096,128]{1,0:T(8,128)(2,1)}) %all-gather.4.cloned.1.call-update) | async-done | bytes 1048592 | tf_op jit(solution)/shard_map/all_gather | solution.py:36
  96.8 5.2 fusion.22
  102.0 5.4 copy.14
  112.1 13.5 %all_gather.19 = bf16[1024,128]{1,0:T(8,128)(2,1)S(1)} all-gather(bf16[128,128]{1,0:T(8,128)(2,1)S(1)} %copy-done.2), channel_id=1, replica_groups=mesh['row'=32,'col'=8] {'col'}, dimensions={0}, use_global_device_ids=true | all-gather | bytes 294912 | tf_op jit(solution)/shard_map/all_gather | solution.py:39
  127.8 4.4 fusion.20
  132.2 5.4 copy.15
  137.6 4.0 fusion.8
  145.6 234.6 %reduce-scatter.9.cloned.1.call-done = f32[128,128]{1,0:T(8,128)} async-done(((f32[4096,128]{1,0:T(8,128)}), f32[128,128]{1,0:T(8,128)}) %reduce-scatter.9.cloned.1.call-update) | async-done | bytes 65552 | tf_op jit(solution)/shard_map/reduce_scatter | solution.py:56
  382.0 73.9 %all-gather.6.cloned.1.call-done = bf16[4096,128]{1,0:T(8,128)(2,1)} async-done(((bf16[128,128]{1,0:T(8,128)(2,1)}), bf16[4096,128]{1,0:T(8,128)(2,1)}) %all-gather.6.cloned.1.call-update) | async-done | bytes 1048592 | tf_op jit(solution)/shard_map/all_gather | solution.py:36
  459.3 5.2 fusion.18
  464.5 5.4 copy.16
  474.6 13.5 %all_gather.21 = bf16[1024,128]{1,0:T(8,128)(2,1)S(1)} all-gather(bf16[128,128]{1,0:T(8,128)(2,1)S(1)} %copy-done.3), channel_id=1, replica_groups=mesh['row'=32,'col'=8] {'col'}, dimensions={0}, use_global_device_ids=true | all-gather | bytes 294912 | tf_op jit(solution)/shard_map/all_gather | solution.py:39
  490.2 4.4 fusion.16
  494.6 5.4 copy.17
  500.1 4.0 fusion.4
  506.8 235.0 %reduce-scatter.13.cloned.1.call-done = f32[128,128]{1,0:T(8,128)} async-done(((f32[4096,128]{1,0:T(8,128)}), f32[128,128]{1,0:T(8,128)}) %reduce-scatter.13.cloned.1.call-update) | async-done | bytes 65552 | tf_op jit(solution)/shard_map/reduce_scatter | solution.py:56
  743.5 74.6 %all-gather.8.cloned.1.call-done = bf16[4096,128]{1,0:T(8,128)(2,1)} async-done(((bf16[128,128]{1,0:T(8,128)(2,1)}), bf16[4096,128]{1,0:T(8,128)(2,1)}) %all-gather.8.cloned.1.call-update) | async-done | bytes 1048592 | tf_op jit(solution)/shard_map/all_gather | solution.py:36
  821.5 5.2 fusion.14
  826.7 5.4 copy.18
  836.8 13.5 %all_gather.23 = bf16[1024,128]{1,0:T(8,128)(2,1)S(1)} all-gather(bf16[128,128]{1,0:T(8,128)(2,1)S(1)} %copy-done.4), channel_id=1, replica_groups=mesh['row'=32,'col'=8] {'col'}, dimensions={0}, use_global_device_ids=true | all-gather | bytes 294912 | tf_op jit(solution)/shard_map/all_gather | solution.py:39
  852.4 4.4 fusion.12
  856.8 5.4 copy.19
  862.3 4.0 fusion
  868.9 235.5 %reduce-scatter.17.cloned.1.call-done = f32[128,128]{1,0:T(8,128)} async-done(((f32[4096,128]{1,0:T(8,128)}), f32[128,128]{1,0:T(8,128)}) %reduce-scatter.17.cloned.1.call-update) | async-done | bytes 65552 | tf_op jit(solution)/shard_map/reduce_scatter | solution.py:56
  (59 shorter events, 46.0 us)
Async XLA Ops:
  6.5 90.3 %copy-start = (bf16[1,1,64,128,128]{4,3,2,1,0:T(8,128)(2,1)S(1)}, bf16[1,1,64,128,128]{4,3,2,1,0:T(8,128)(2,1)}, u32[]{:S(2)}) copy-start(bf16[1,1,64,128,128]{4,3,2,1,0:T(8,128)(2,1)} %param.7) | copy-start | bytes 6291460
  6.5 86.9 %all-gather.4.cloned.1.call-start = ((), (), s32[]{:S(2)}) async-start(), calls=%async_computation.6 | async-start | bytes 1081344 | tf_op jit(solution)/shard_map/all_gather | solution.py:36
  8.2 137.4 %reduce-scatter.7.cloned.1.call-start = ((), (), s32[]{:S(2)}) async-start(), calls=%async_computation.7 | async-start | bytes 589824 | tf_op jit(solution)/shard_map/reduce_scatter | solution.py:49
  102.0 5.4 copy-start.5
  107.4 4.7 copy-start.2
  112.0 268.2 %reduce-scatter.9.cloned.1.call-start = ((), (), s32[]{:S(2)}) async-start(), calls=%async_computation.8 | async-start | bytes 2162688 | tf_op jit(solution)/shard_map/reduce_scatter | solution.py:56
  132.2 5.4 copy-start.6
  144.2 236.0 %copy-start.1 = (f32[128,128]{1,0:T(8,128)S(1)}, f32[128,128]{1,0:T(8,128)}, u32[]{:S(2)}) copy-start(f32[128,128]{1,0:T(8,128)} %param.11) | copy-start | bytes 196612
  144.2 311.7 %all-gather.6.cloned.1.call-start = ((), (), s32[]{:S(2)}) async-start(), calls=%async_computation.9 | async-start | bytes 1081344 | tf_op jit(solution)/shard_map/all_gather | solution.py:36
  381.8 125.0 %reduce-scatter.11.cloned.1.call-start = ((), (), s32[]{:S(2)}) async-start(), calls=%async_computation.10 | async-start | bytes 589824 | tf_op jit(solution)/shard_map/reduce_scatter | solution.py:49
  469.9 4.7 copy-start.3
  474.5 267.2 %reduce-scatter.13.cloned.1.call-start = ((), (), s32[]{:S(2)}) async-start(), calls=%async_computation.11 | async-start | bytes 2162688 | tf_op jit(solution)/shard_map/reduce_scatter | solution.py:56
  506.7 311.4 %all-gather.8.cloned.1.call-start = ((), (), s32[]{:S(2)}) async-start(), calls=%async_computation.12 | async-start | bytes 1081344 | tf_op jit(solution)/shard_map/all_gather | solution.py:36
  743.2 125.7 %reduce-scatter.15.cloned.1.call-start = ((), (), s32[]{:S(2)}) async-start(), calls=%async_computation.13 | async-start | bytes 589824 | tf_op jit(solution)/shard_map/reduce_scatter | solution.py:49
  832.1 4.7 copy-start.4
  836.7 267.8 %reduce-scatter.17.cloned.1.call-start = ((), (), s32[]{:S(2)}) async-start(), calls=%async_computation.14 | async-start | bytes 2162688 | tf_op jit(solution)/shard_map/reduce_scatter | solution.py:56
Sparse Core Ops, SparseCore 0:
  10.7 82.6 all-gather.3
  112.1 28.7 reduce-scatter.6
  144.4 235.8 reduce-scatter.8
  383.5 72.3 all-gather.5
  474.6 28.6 reduce-scatter.10
  506.8 234.8 reduce-scatter.12
  745.1 72.9 all-gather.7
  836.8 28.6 reduce-scatter.14
  869.0 235.3 reduce-scatter.16
where the time goes:
time: 1110 us
  waiting for transfers between devices  938 us (85%)
  local copies, waits for them, and re-layouts  59.8 us (5%)
  matrix products  51.8 us (5%)
  blocking collectives  40.5 us (4%)
  between operations  15.3 us (1%)
    reduce_scatter x3, waiting for transfers between devices, body(): lax.psum_scatter(lower_partial.reshape(-1, vectors), 'row', scatter_dimen...  705 us
    all_gather x3, waiting for transfers between devices, body(): lax.all_gather(panel, 'row', axis=0, tiled=True)  232 us
    all_gather x3, blocking collectives, body(): lax.all_gather(panel, 'col', axis=0, tiled=True)  40.5 us
  transfers between devices with their start and end apart: 9, of which 6 were waited for; matrix products, arithmetic and copies ran while one was open for 5% of the time, Pallas kernels for 0%

commit v1 on v0

v1 whole, which is shorter than its diff:
```python
import jax
import jax.numpy as jnp
from jax import lax
from jax.experimental import pallas as pl
from jax.experimental.pallas import tpu as pltpu
from jax.sharding import PartitionSpec as P

DEGREE = 3
RING = 4
HALVES = 2
F32 = jnp.float32
BF16 = jnp.bfloat16
MESH = pl.DeviceIdType.MESH
GROUP = 8

P2T = BF16
ZT = BF16
U1T = F32
U2T = BF16


def plan(slots, row_count, col_count):
    names = {}
    at = 0
    for name, size in (
        ("u_block", slots),
        ("u_panel", slots),
        ("u_keep", slots),
        ("u_end", row_count),
        ("l_block", slots),
        ("l_panel", slots),
        ("l_keep", slots),
        ("l_end", col_count),
    ):
        names[name] = at
        at += size
    return names


def order(key, payload, live, segments):
    slots = key.shape[0]
    slot = jnp.arange(slots, dtype=jnp.int32)
    key = jnp.where(live, key, segments)
    payload = jnp.where(live, payload, 0)
    before = (key[None, :] < key[:, None]) | (
        (key[None, :] == key[:, None]) & (slot[None, :] < slot[:, None])
    )
    rank = jnp.sum(before.astype(jnp.int32), axis=1)
    hit = (rank[None, :] == slot[:, None]).astype(jnp.int32)
    block = jnp.sum(hit * slot[None, :], axis=1)
    panel = jnp.sum(hit * payload[None, :], axis=1)
    sorted_key = jnp.sum(hit * key[None, :], axis=1)
    keep = (sorted_key == jnp.roll(sorted_key, 1)) & (slot > 0)
    segment = jnp.arange(segments, dtype=jnp.int32)
    upto = jnp.sum((key[None, :] <= segment[:, None]).astype(jnp.int32), axis=1)
    have = jnp.sum((key[None, :] == segment[:, None]).astype(jnp.int32), axis=1)
    end = jnp.where(have > 0, upto, 0)
    return [block, panel, keep.astype(jnp.int32), end]


def kernel(
    at,
    meta,
    center,
    halfwidth,
    blocks_hbm,
    initial,
    out,
    blocks,
    current,
    previous,
    col0,
    col1,
    col2,
    row0,
    row1,
    row2,
    ups,
    lows,
    lsend,
    comb,
    r1opp,
    r1,
    msum,
    msend,
    r2,
    zsend,
    rz,
    usend1,
    ru1,
    usend2,
    ru2,
    load_sem,
    ssem,
    rsem,
):
    slots = blocks.shape[0]
    half = current.shape[0] // 2
    grid_row = lax.axis_index("row")
    grid_col = lax.axis_index("col")
    core = grid_col % 2
    zl = grid_col // 2
    zh = grid_row % HALVES
    x = grid_row // HALVES % RING
    y = grid_row // (HALVES * RING)
    a = x * (1 - core) + y * core
    b = y * (1 - core) + x * core

    def place(da=0, db=0, dh=0, dz=0):
        pa, pb = (a + da) % RING, (b + db) % RING
        px = pa * (1 - core) + pb * core
        py = pb * (1 - core) + pa * core
        return (
            (py * RING + px) * HALVES + (zh + dh) % HALVES,
            (zl + dz) % RING * 2 + core,
        )

    other_core = (grid_row, zl * 2 + 1 - core)

    load = pltpu.make_async_copy(blocks_hbm, blocks, load_sem)
    load.start()

    barrier = pltpu.get_barrier_semaphore()
    peers = [other_core, place(dh=1)]
    peers += [place(da=d) for d in (1, 2, 3)]
    peers += [place(db=d) for d in (1, 2, 3)]
    peers += [place(dz=d) for d in (1, 2, 3)]
    for peer in peers:
        pl.semaphore_signal(barrier, inc=1, device_id=peer, device_id_type=MESH)
    current[...] = initial[...]
    ups[0] = jnp.zeros_like(initial)
    lows[0] = jnp.zeros_like(initial)
    pl.semaphore_wait(barrier, len(peers))

    ids = {}
    sent = []

    def copy(s, name, src, dst, device):
        index = ids.setdefault(name, len(ids))
        return pltpu.make_async_remote_copy(
            src_ref=src,
            dst_ref=dst,
            send_sem=ssem.at[s, index],
            recv_sem=rsem.at[s, index],
            device_id=device,
            device_id_type=MESH,
        )

    def slot_of(da=0, db=0, dh=0):
        return ((b + db) % RING * RING + (a + da) % RING) * HALVES + (zh + dh) % HALVES

    top, bottom = pl.ds(0, half), pl.ds(half, half)

    def step(s):
        col, row = (col0, col1, col2)[s], (row0, row1, row2)[s]

        def send(name, src, dst, device):
            sent.append((s, name, src))
            copy(s, name, src, dst, device).start()

        def wait(name, dst):
            copy(s, name, dst, dst, other_core).wait_recv()

        def panel(da=0, db=0, dh=0):
            return col.at[slot_of(da, db, dh)]

        def spread1(dh):
            for d in (2, 1, 3):
                send(f"d1.{dh}.{d}", panel(dh=dh), panel(dh=dh), place(da=d))

        def got1(dh, d):
            wait(f"d1.{dh}.{d}", panel(da=-d, dh=dh))

        def spread2(dh, d):
            for side, go in ((0, 1), (1, 3)):
                send(
                    f"d2.{dh}.{d}.{side}",
                    panel(da=-d, dh=dh),
                    panel(da=-d, dh=dh),
                    place(db=go),
                )

        def relay2(dh, d):
            for side, go, part in ((0, 1, top), (1, 3, bottom)):
                have = panel(da=-d, db=-go, dh=dh)
                wait(f"d2.{dh}.{d}.{side}", have)
                send(
                    f"far.{dh}.{d}.{side}",
                    panel(da=-d, db=-go, dh=dh).at[part],
                    have.at[part],
                    place(db=go),
                )

        def far2(dh, d):
            for side, part in ((0, top), (1, bottom)):
                wait(f"far.{dh}.{d}.{side}", panel(da=-d, db=2, dh=dh).at[part])

        def row_at(dz, which):
            return row.at[(zl + dz) % RING * 2 + which]

        def row_pass(d):
            wait(f"row.{d}", row_at(-d, core))
            send(f"pass.{d}", row_at(-d, core), row_at(-d, core), other_core)

        def low_end(ra, rb, dh):
            return meta[at["l_end"] + slot_of(ra, rb, dh)]

        def reduce1_start(dh):
            for rb in range(RING):
                far = low_end(2, rb, dh)
                lsend[s, dh, 0, rb] = lows[far, top, :].astype(BF16)
                lsend[s, dh, 1, rb] = lows[far, bottom, :].astype(BF16)
            send(f"opp.{dh}.0", lsend.at[s, dh, 0], r1opp.at[s, dh, 0], place(da=1))
            send(f"opp.{dh}.1", lsend.at[s, dh, 1], r1opp.at[s, dh, 1], place(da=3))
            for rb in range(RING):
                lsend[s, dh, 2, rb] = lows[low_end(1, rb, dh), bottom, :].astype(BF16)
                lsend[s, dh, 3, rb] = lows[low_end(3, rb, dh), top, :].astype(BF16)
            send(f"near.{dh}.0", lsend.at[s, dh, 2], r1.at[s, dh, 0, 1], place(da=1))
            send(f"near.{dh}.1", lsend.at[s, dh, 3], r1.at[s, dh, 1, 0], place(da=3))

        def reduce1_join(dh):
            for side, go, part in ((0, 1, top), (1, 3, bottom)):
                wait(f"opp.{dh}.{side}", r1opp.at[s, dh, side])
                for rb in range(RING):
                    mine = lows[low_end(go, rb, dh), part, :]
                    comb[s, dh, side, rb] = (mine + r1opp[s, dh, side, rb].astype(F32)).astype(BF16)
                send(
                    f"join.{dh}.{side}",
                    comb.at[s, dh, side],
                    r1.at[s, dh, side, side],
                    place(da=go),
                )

        def reduce1_end(dh):
            wait(f"near.{dh}.0", r1.at[s, dh, 0, 1])
            wait(f"near.{dh}.1", r1.at[s, dh, 1, 0])
            wait(f"join.{dh}.0", r1.at[s, dh, 0, 0])
            wait(f"join.{dh}.1", r1.at[s, dh, 1, 1])
            for rb in (2, 1, 3, 0):
                mine = low_end(0, rb, dh)
                for which, part in ((0, top), (1, bottom)):
                    total = (
                        lows[mine, part, :]
                        + r1[s, dh, 0, which, rb].astype(F32)
                        + r1[s, dh, 1, which, rb].astype(F32)
                    )
                    if rb == 0:
                        msum[dh, part, :] = total
                    else:
                        msend[s, dh, rb - 1, part, :] = total.astype(P2T)
                if rb:
                    send(
                        f"mid.{dh}.{rb}",
                        msend.at[s, dh, rb - 1],
                        r2.at[s, dh, rb - 1],
                        place(db=rb),
                    )

        def reduce2_end(dh):
            total = msum[dh]
            for rb in (1, 3, 2):
                wait(f"mid.{dh}.{rb}", r2.at[s, dh, rb - 1])
                total = total + r2[s, dh, rb - 1].astype(F32)
            return total

        now = current[...]
        col[slot_of()] = now.astype(BF16)
        send("z", panel(), panel(), place(dh=1))
        spread1(0)
        spread2(0, 0)
        row[grid_col] = now.T.astype(BF16)
        for d in (2, 1, 3):
            send(f"row.{d}", row_at(0, core), row_at(0, core), place(dz=d))
        send("swap", row_at(0, core), row_at(0, core), other_core)

        got1(0, 1)
        spread2(0, 1)
        got1(0, 3)
        spread2(0, 3)
        relay2(0, 0)
        got1(0, 2)
        spread2(0, 2)
        row_pass(1)
        row_pass(3)
        row_pass(2)
        relay2(0, 1)
        relay2(0, 3)
        wait("z", panel(dh=1))
        spread1(1)
        spread2(1, 0)
        relay2(0, 2)
        wait("swap", row_at(0, 1 - core))
        for d in (1, 3, 2):
            wait(f"pass.{d}", row_at(-d, 1 - core))

        if s == 0:
            load.wait()

        @pl.loop(0, slots // GROUP)
        def _(g):
            total = lows[g * GROUP]
            for i in range(GROUP):
                k = g * GROUP + i
                product = jnp.dot(
                    row[meta[at["l_panel"] + k]],
                    blocks[meta[at["l_block"] + k]],
                    preferred_element_type=F32,
                )
                total = product + meta[at["l_keep"] + k].astype(F32) * total
                lows[k + 1] = total

        reduce1_start(1)
        got1(1, 1)
        spread2(1, 1)
        got1(1, 3)
        spread2(1, 3)
        relay2(1, 0)
        got1(1, 2)
        spread2(1, 2)
        reduce1_start(0)
        relay2(1, 1)
        relay2(1, 3)
        reduce1_join(1)
        relay2(1, 2)
        reduce1_join(0)
        reduce1_end(1)
        for dh in (0, 1):
            for d in (0, 1, 3, 2):
                far2(dh, d)

        @pl.loop(0, slots // GROUP)
        def _(g):
            total = ups[g * GROUP]
            for i in range(GROUP):
                k = g * GROUP + i
                product = jnp.dot(
                    blocks[meta[at["u_block"] + k]],
                    col[meta[at["u_panel"] + k]],
                    preferred_element_type=F32,
                )
                total = product + meta[at["u_keep"] + k].astype(F32) * total
                ups[k + 1] = total

        def up_end(dz, which):
            return meta[at["u_end"] + (zl + dz) % RING * 2 + which]

        for d in range(RING):
            usend1[s, d] = ups[up_end(d, 1 - core)].astype(U1T)
        send("chip", usend1.at[s], ru1.at[s], other_core)
        zsend[s] = reduce2_end(1).astype(ZT)
        send("back", zsend.at[s], rz.at[s], place(dh=1))
        reduce1_end(0)
        wait("chip", ru1.at[s])
        for d in (2, 1, 3):
            usend2[s, d - 1] = (ups[up_end(d, core)] + ru1[s, d].astype(F32)).astype(U2T)
            send(f"up.{d}", usend2.at[s, d - 1], ru2.at[s, d - 1], place(dz=d))
        upper = ups[up_end(0, core)] + ru1[s, 0].astype(F32)
        lower = reduce2_end(0)
        for d in (1, 3, 2):
            wait(f"up.{d}", ru2.at[s, d - 1])
            upper = upper + ru2[s, d - 1].astype(F32)
        wait("back", rz.at[s])
        lower = lower + rz[s].astype(F32)
        applied = upper + lower.T
        shifted = (applied - center[0] * now) / halfwidth[0]
        following = shifted if s == 0 else 2.0 * shifted - previous[...]
        previous[...] = now
        current[...] = following

    for s in range(DEGREE):
        step(s)

    for s, name, src in sent:
        copy(s, name, src, src, other_core).wait_send()

    out[...] = current[...]


def body(hamiltonian_blocks, block_rows, block_cols, block_counts, initial, center, halfwidth):
    stacked = hamiltonian_blocks[0, 0]
    slots, orbitals, _ = stacked.shape
    vectors = initial.shape[1]
    row_count = lax.axis_size("col")
    col_count = lax.axis_size("row")
    at = plan(slots, row_count, col_count)
    core = lax.axis_index("col") % 2
    rows, cols = block_rows[0, 0], block_cols[0, 0]
    live = jnp.arange(slots, dtype=jnp.int32) < block_counts[0, 0]
    chip = cols // HALVES
    turned = (chip % RING * RING + chip // RING) * HALVES + cols % HALVES
    cols = jnp.where(core == 0, cols, turned)
    meta = jnp.concatenate(
        order(rows, cols, live, row_count) + order(cols, rows, live, col_count)
    )

    steps = DEGREE
    square = (orbitals, vectors)
    part = (orbitals // 2, vectors)
    copies = 69
    vmem = pltpu.VMEM
    scratch = [
        vmem((slots, orbitals, orbitals), BF16),
        vmem(square, F32),
        vmem(square, F32),
        *[vmem((col_count,) + square, BF16)] * steps,
        *[vmem((row_count,) + square, BF16)] * steps,
        vmem((slots + 1,) + square, F32),
        vmem((slots + 1,) + square, F32),
        vmem((steps, 2, 4, RING) + part, BF16),
        vmem((steps, 2, 2, RING) + part, BF16),
        vmem((steps, 2, 2, RING) + part, BF16),
        vmem((steps, 2, 2, 2, RING) + part, BF16),
        vmem((2,) + square, F32),
        vmem((steps, 2, RING - 1) + square, P2T),
        vmem((steps, 2, RING - 1) + square, P2T),
        vmem((steps,) + square, ZT),
        vmem((steps,) + square, ZT),
        vmem((steps, RING) + square, U1T),
        vmem((steps, RING) + square, U1T),
        vmem((steps, RING - 1) + square, U2T),
        vmem((steps, RING - 1) + square, U2T),
        pltpu.SemaphoreType.DMA,
        pltpu.SemaphoreType.DMA((steps, copies)),
        pltpu.SemaphoreType.DMA((steps, copies)),
    ]
    smem = pl.BlockSpec(memory_space=pltpu.SMEM)
    whole = pl.BlockSpec(memory_space=pltpu.VMEM)

    def run(*refs):
        kernel(at, *refs)

    return pl.pallas_call(
        run,
        out_shape=jax.ShapeDtypeStruct(square, F32),
        in_specs=[smem, smem, smem, pl.BlockSpec(memory_space=pl.ANY), whole],
        out_specs=whole,
        scratch_shapes=scratch,
        compiler_params=pltpu.CompilerParams(collective_id=0, has_side_effects=True),
        name="filter",
    )(meta, center, halfwidth, stacked, initial)


def solution(mesh):
    in_specs = (
        P("row", "col", None, None, None),
        P("row", "col", None),
        P("row", "col", None),
        P("row", "col"),
        P(("row", "col"), None),
        P(),
        P(),
    )
    out_specs = P(("row", "col"), None)
    return jax.shard_map(body, mesh=mesh, in_specs=in_specs, out_specs=out_specs, check_vma=False)
```

time: 1110 us -> 109 us (0.10)
  the two profiles are of different devices: /device:TPU:32 before, /device:TPU:1 now
where the time goes in v1:
time: 109 us
  Pallas kernels  100 us (92%)
  local copies, waits for them, and re-layouts  3.32 us (3%)
  other arithmetic  3.07 us (3%)
  between operations  1.98 us (2%)
    pallas_call x1, Pallas kernels, body(): pl.pallas_call(run, out_shape=jax.ShapeDtypeStruct(square, F32), in_specs...  100 us

profile of v1, /device:TPU:1, one launch (start us, length us, event | category | flops | bytes accessed | tf_op | source)
XLA Modules:
  0.0 108.8 jit_solution(3839595917091615099)
XLA Ops:
  1.9 0.7 bitcast_select_fusion
  2.7 0.2 convert_reduce_fusion.1
  2.8 0.2 convert_reduce_fusion
  3.0 0.2 select_reduce_fusion
  3.2 0.6 slice.16
  3.8 0.7 and_convert_fusion
  4.5 0.1 select_reduce_fusion.3
  4.6 0.6 slice.14
  5.2 0.7 and_convert_fusion.1
  5.9 0.1 convert_reduce_fusion.5
  6.1 0.1 convert_reduce_fusion.3
  6.2 0.7 concatenate.12.refs_0_
  6.9 100.4 %filter.1 = f32[128,128]{1,0:T(8,128)} custom-call(s32[424]{0:T(512)} %concatenate.12.refs_0_, f32[1]{0:T(128)S(6)} %copy.10.refs_1_, f32[1]{0:T(128)S(6)} %copy.11.refs_2_, bf16[64,128,128]{2,1,0:T(8,128)(2,1)} %bitcast.24, f32[128,128]{1,0:T(8,128)} %refs_4_.1), custom_call_target="tpu_custom_call" | custom-call | tf_op jit(solution)/shard_map/filter/pallas_call | solution.py:432
  107.3 1.5 %copy.12 = f32[128,128]{1,0:T(8,128)} copy(f32[128,128]{1,0:T(8,128)} %filter.1) | data formatting | bytes 131072
  (3 shorter events, 0.0 us)

commit v2 on v1

v2 whole, which is shorter than its diff:
```python
import jax
import jax.numpy as jnp
from jax import lax
from jax.experimental import pallas as pl
from jax.experimental.pallas import tpu as pltpu
from jax.sharding import PartitionSpec as P

DEGREE = 3
RING = 4
HALVES = 2
F32 = jnp.float32
BF16 = jnp.bfloat16
MESH = pl.DeviceIdType.MESH
GROUP = 32
AWAY = (2, 1, 3)

LT = BF16
MT = BF16
ZT = BF16
U1T = F32
U2T = BF16


def plan(slots, row_count, col_count):
    names = {}
    at = 0
    for name, size in (
        ("u_block", slots),
        ("u_panel", slots),
        ("u_keep", slots),
        ("u_end", row_count),
        ("l_block", slots),
        ("l_panel", slots),
        ("l_keep", slots),
        ("l_end", col_count),
    ):
        names[name] = at
        at += size
    return names


def order(key, payload, live, segments):
    slots = key.shape[0]
    slot = jnp.arange(slots, dtype=jnp.int32)
    key = jnp.where(live, key, segments)
    payload = jnp.where(live, payload, 0)
    before = (key[None, :] < key[:, None]) | (
        (key[None, :] == key[:, None]) & (slot[None, :] < slot[:, None])
    )
    rank = jnp.sum(before.astype(jnp.int32), axis=1)
    hit = (rank[None, :] == slot[:, None]).astype(jnp.int32)
    block = jnp.sum(hit * slot[None, :], axis=1)
    panel = jnp.sum(hit * payload[None, :], axis=1)
    sorted_key = jnp.sum(hit * key[None, :], axis=1)
    keep = (sorted_key == jnp.roll(sorted_key, 1)) & (slot > 0)
    segment = jnp.arange(segments, dtype=jnp.int32)
    upto = jnp.sum((key[None, :] <= segment[:, None]).astype(jnp.int32), axis=1)
    have = jnp.sum((key[None, :] == segment[:, None]).astype(jnp.int32), axis=1)
    end = jnp.where(have > 0, upto, 0)
    return [block, panel, keep.astype(jnp.int32), end]


def kernel(
    at,
    meta,
    center,
    halfwidth,
    blocks_hbm,
    initial,
    out,
    blocks,
    current,
    previous,
    col0,
    col1,
    col2,
    row0,
    row1,
    row2,
    ups,
    lows,
    lsend,
    r1,
    msum,
    msend,
    r2,
    zsend,
    rz,
    usend1,
    ru1,
    usend2,
    ru2,
    load_sem,
    ssem,
    rsem,
):
    slots = blocks.shape[0]
    grid_row = lax.axis_index("row")
    grid_col = lax.axis_index("col")
    core = grid_col % 2
    zl = grid_col // 2
    zh = grid_row % HALVES
    x = grid_row // HALVES % RING
    y = grid_row // (HALVES * RING)

    a = x * (1 - core) + y * core
    b = y * (1 - core) + x * core

    def row_of(da=0, db=0, dh=0):
        pa, pb = (a + da) % RING, (b + db) % RING
        px = pa * (1 - core) + pb * core
        py = pb * (1 - core) + pa * core
        return (py * RING + px) * HALVES + (zh + dh) % HALVES

    def place(da=0, db=0, dh=0, dz=0):
        return (row_of(da, db, dh), (zl + dz) % RING * 2 + core)

    other_core = (grid_row, zl * 2 + 1 - core)

    load = pltpu.make_async_copy(blocks_hbm, blocks, load_sem)
    load.start()

    barrier = pltpu.get_barrier_semaphore()
    peers = [other_core, place(dh=1)]
    peers += [place(da=d) for d in AWAY] + [place(db=d) for d in AWAY]
    peers += [place(dz=d) for d in AWAY]
    for peer in peers:
        pl.semaphore_signal(barrier, inc=1, device_id=peer, device_id_type=MESH)
    current[...] = initial[...]
    ups[0] = jnp.zeros_like(initial)
    lows[0] = jnp.zeros_like(initial)
    pl.semaphore_wait(barrier, len(peers))

    ids = {}
    sent = []

    def copy(s, name, src, dst, device):
        index = ids.setdefault(name, len(ids))
        return pltpu.make_async_remote_copy(
            src_ref=src,
            dst_ref=dst,
            send_sem=ssem.at[s, index],
            recv_sem=rsem.at[s, index],
            device_id=device,
            device_id_type=MESH,
        )

    def step(s):
        col, row = (col0, col1, col2)[s], (row0, row1, row2)[s]

        def send(name, src, dst, device):
            sent.append((s, name, src))
            copy(s, name, src, dst, device).start()

        def wait(name, dst):
            copy(s, name, dst, dst, other_core).wait_recv()

        def panel(da=0, db=0, dh=0):
            return col.at[row_of(da, db, dh)]

        def spread1(dh):
            for d in AWAY:
                send(f"d1.{dh}.{d}", panel(dh=dh), panel(dh=dh), place(da=d))

        def spread2(dh, da):
            for d in AWAY:
                held = panel(da=-da, dh=dh)
                send(f"d2.{dh}.{da}.{d}", held, held, place(db=d))

        def pass2(dh, da):
            wait(f"d1.{dh}.{da}", panel(da=-da, dh=dh))
            spread2(dh, da)

        def row_at(dz, which):
            return row.at[(zl + dz) % RING * 2 + which]

        def low_end(da, db, dh):
            return meta[at["l_end"] + row_of(da, db, dh)]

        def reduce1_start(dh):
            for db in AWAY + (0,):
                for d in AWAY:
                    lsend[s, dh, db, d - 1] = lows[low_end(d, db, dh)].astype(LT)
                    send(
                        f"low.{dh}.{db}.{d}",
                        lsend.at[s, dh, db, d - 1],
                        r1.at[s, dh, db, d - 1],
                        place(da=d),
                    )

        def reduce1_end(dh, db):
            total = lows[low_end(0, db, dh)]
            for d in (1, 3, 2):
                wait(f"low.{dh}.{db}.{d}", r1.at[s, dh, db, d - 1])
                total = total + r1[s, dh, db, d - 1].astype(F32)
            if db == 0:
                msum[dh] = total
            else:
                msend[s, dh, db - 1] = total.astype(MT)
                send(f"mid.{dh}.{db}", msend.at[s, dh, db - 1], r2.at[s, dh, db - 1], place(db=db))

        def reduce2_end(dh):
            total = msum[dh]
            for d in (1, 3, 2):
                wait(f"mid.{dh}.{d}", r2.at[s, dh, d - 1])
                total = total + r2[s, dh, d - 1].astype(F32)
            return total

        now = current[...]
        col[row_of()] = now.astype(BF16)
        send("z", panel(), panel(), place(dh=1))
        row[grid_col] = now.T.astype(BF16)
        for d in (2, 1, 3):
            send(f"row.{d}", row_at(0, core), row_at(0, core), place(dz=d))
        send("swap", row_at(0, core), row_at(0, core), other_core)
        spread1(0)
        spread2(0, 0)
        pass2(0, 1)
        pass2(0, 3)
        for d in (1, 3):
            wait(f"row.{d}", row_at(-d, core))
            send(f"pass.{d}", row_at(-d, core), row_at(-d, core), other_core)
        pass2(0, 2)
        for d in (2,):
            wait(f"row.{d}", row_at(-d, core))
            send(f"pass.{d}", row_at(-d, core), row_at(-d, core), other_core)
        wait("z", panel(dh=1))
        spread1(1)
        spread2(1, 0)
        wait("swap", row_at(0, 1 - core))
        for d in (1, 3, 2):
            wait(f"pass.{d}", row_at(-d, 1 - core))
        if s == 0:
            load.wait()

        @pl.loop(0, slots // GROUP)
        def _(g):
            total = lows[g * GROUP]
            for i in range(GROUP):
                k = g * GROUP + i
                product = jnp.dot(
                    row[meta[at["l_panel"] + k]],
                    blocks[meta[at["l_block"] + k]],
                    preferred_element_type=F32,
                )
                total = product + meta[at["l_keep"] + k].astype(F32) * total
                lows[k + 1] = total

        reduce1_start(1)
        pass2(1, 1)
        pass2(1, 3)
        pass2(1, 2)
        reduce1_start(0)
        for db in AWAY + (0,):
            reduce1_end(1, db)
        for dh in (0, 1):
            for da in (0, 1, 3, 2):
                for d in (1, 3, 2):
                    wait(f"d2.{dh}.{da}.{d}", panel(-da, -d, dh))

        @pl.loop(0, slots // GROUP)
        def _(g):
            total = ups[g * GROUP]
            for i in range(GROUP):
                k = g * GROUP + i
                product = jnp.dot(
                    blocks[meta[at["u_block"] + k]],
                    col[meta[at["u_panel"] + k]],
                    preferred_element_type=F32,
                )
                total = product + meta[at["u_keep"] + k].astype(F32) * total
                ups[k + 1] = total

        def up_end(dz, which):
            return meta[at["u_end"] + (zl + dz) % RING * 2 + which]

        for d in range(RING):
            usend1[s, d] = ups[up_end(d, 1 - core)].astype(U1T)
        send("chip", usend1.at[s], ru1.at[s], other_core)
        zsend[s] = reduce2_end(1).astype(ZT)
        send("back", zsend.at[s], rz.at[s], place(dh=1))
        wait("chip", ru1.at[s])
        for d in (2, 1, 3):
            usend2[s, d - 1] = (ups[up_end(d, core)] + ru1[s, d].astype(F32)).astype(U2T)
            send(f"up.{d}", usend2.at[s, d - 1], ru2.at[s, d - 1], place(dz=d))
        upper = ups[up_end(0, core)] + ru1[s, 0].astype(F32)
        for db in AWAY + (0,):
            reduce1_end(0, db)
        lower = reduce2_end(0)
        for d in (1, 3, 2):
            wait(f"up.{d}", ru2.at[s, d - 1])
            upper = upper + ru2[s, d - 1].astype(F32)
        wait("back", rz.at[s])
        lower = lower + rz[s].astype(F32)
        applied = upper + lower.T
        shifted = (applied - center[0] * now) / halfwidth[0]
        following = shifted if s == 0 else 2.0 * shifted - previous[...]
        previous[...] = now
        current[...] = following

    for s in range(DEGREE):
        step(s)

    for s, name, src in sent:
        copy(s, name, src, src, other_core).wait_send()

    out[...] = current[...]


def body(hamiltonian_blocks, block_rows, block_cols, block_counts, initial, center, halfwidth):
    stacked = hamiltonian_blocks[0, 0]
    slots, orbitals, _ = stacked.shape
    vectors = initial.shape[1]
    row_count = lax.axis_size("col")
    col_count = lax.axis_size("row")
    at = plan(slots, row_count, col_count)
    rows, cols = block_rows[0, 0], block_cols[0, 0]
    live = jnp.arange(slots, dtype=jnp.int32) < block_counts[0, 0]
    meta = jnp.concatenate(
        order(rows, cols, live, row_count) + order(cols, rows, live, col_count)
    )

    steps = DEGREE
    square = (orbitals, vectors)
    copies = 73
    vmem = pltpu.VMEM
    scratch = [
        vmem((slots, orbitals, orbitals), BF16),
        vmem(square, F32),
        vmem(square, F32),
        *[vmem((col_count,) + square, BF16)] * steps,
        *[vmem((row_count,) + square, BF16)] * steps,
        vmem((slots + 1,) + square, F32),
        vmem((slots + 1,) + square, F32),
        vmem((steps, 2, RING, RING - 1) + square, LT),
        vmem((steps, 2, RING, RING - 1) + square, LT),
        vmem((2,) + square, F32),
        vmem((steps, 2, RING - 1) + square, MT),
        vmem((steps, 2, RING - 1) + square, MT),
        vmem((steps,) + square, ZT),
        vmem((steps,) + square, ZT),
        vmem((steps, RING) + square, U1T),
        vmem((steps, RING) + square, U1T),
        vmem((steps, RING - 1) + square, U2T),
        vmem((steps, RING - 1) + square, U2T),
        pltpu.SemaphoreType.DMA,
        pltpu.SemaphoreType.DMA((steps, copies)),
        pltpu.SemaphoreType.DMA((steps, copies)),
    ]
    smem = pl.BlockSpec(memory_space=pltpu.SMEM)
    whole = pl.BlockSpec(memory_space=pltpu.VMEM)

    def run(*refs):
        kernel(at, *refs)

    return pl.pallas_call(
        run,
        out_shape=jax.ShapeDtypeStruct(square, F32),
        in_specs=[smem, smem, smem, pl.BlockSpec(memory_space=pl.ANY), whole],
        out_specs=whole,
        scratch_shapes=scratch,
        compiler_params=pltpu.CompilerParams(collective_id=0, has_side_effects=True),
        name="filter",
    )(meta, center, halfwidth, stacked, initial)


def solution(mesh):
    in_specs = (
        P("row", "col", None, None, None),
        P("row", "col", None),
        P("row", "col", None),
        P("row", "col"),
        P(("row", "col"), None),
        P(),
        P(),
    )
    out_specs = P(("row", "col"), None)
    return jax.shard_map(body, mesh=mesh, in_specs=in_specs, out_specs=out_specs, check_vma=False)
```

time: 109 us -> 98.5 us (0.904)
  Pallas kernels: 100 us -> 89.9 us
    pallas_call x1, Pallas kernels: 100 us -> 89.9 us  [body(): pl.pallas_call(run, out_shape=jax.ShapeDtypeStruct(square, F32), in_specs...]
where the time goes in v2:
time: 98.5 us; the launch traced here: 98.3 us
  Pallas kernels  89.9 us (91%)
  local copies, waits for them, and re-layouts  3.32 us (3%)
  other arithmetic  3.05 us (3%)
  between operations  1.97 us (2%)
    pallas_call x1, Pallas kernels, body(): pl.pallas_call(run, out_shape=jax.ShapeDtypeStruct(square, F32), in_specs...  89.9 us

profile of v2, /device:TPU:1, one launch (start us, length us, event | category | flops | bytes accessed | tf_op | source)
XLA Modules:
  0.0 98.3 jit_solution(9409191997900635489)
XLA Ops:
  1.9 0.7 bitcast_select_fusion
  2.6 0.2 convert_reduce_fusion
  2.8 0.2 convert_reduce_fusion.1
  3.0 0.2 select_reduce_fusion.3
  3.1 0.6 slice.14
  3.7 0.7 and_convert_fusion.1
  4.4 0.1 select_reduce_fusion
  4.6 0.6 slice.16
  5.2 0.7 and_convert_fusion
  5.9 0.1 convert_reduce_fusion.3
  6.0 0.1 convert_reduce_fusion.5
  6.2 0.7 concatenate.12.refs_0_
  6.9 89.9 %filter.1 = f32[128,128]{1,0:T(8,128)} custom-call(s32[424]{0:T(512)} %concatenate.12.refs_0_, f32[1]{0:T(128)S(6)} %copy.10.refs_1_, f32[1]{0:T(128)S(6)} %copy.11.refs_2_, bf16[64,128,128]{2,1,0:T(8,128)(2,1)} %bitcast.11, f32[128,128]{1,0:T(8,128)} %refs_4_.1), custom_call_target="tpu_custom_call" | custom-call | tf_op jit(solution)/shard_map/filter/pallas_call | solution.py:356
  96.8 1.5 %copy.12 = f32[128,128]{1,0:T(8,128)} copy(f32[128,128]{1,0:T(8,128)} %filter.1) | data formatting | bytes 131072
  (2 shorter events, 0.0 us)

commit v3 on v2

v3 whole, which is shorter than its diff:
```python
import jax
import jax.numpy as jnp
from jax import lax
from jax.experimental import pallas as pl
from jax.experimental.pallas import tpu as pltpu
from jax.sharding import PartitionSpec as P

DEGREE = 3
RING = 4
HALVES = 2
F32 = jnp.float32
BF16 = jnp.bfloat16
MESH = pl.DeviceIdType.MESH
GROUP = 32
AWAY = (2, 1, 3)

LT = BF16
MT = BF16
ZT = BF16
U1T = F32
U2T = BF16


U_BLOCK, U_PANEL, U_KEEP, U_END, L_BLOCK, L_PANEL, L_KEEP, L_END = range(8)


def order(key, payload, live, segments):
    slots = key.shape[1]
    square = (slots, slots)
    lane = lax.broadcasted_iota(jnp.int32, square, 1)
    slot = lax.broadcasted_iota(jnp.int32, square, 0)

    def upright(v):
        return jnp.sum(jnp.where(lane == slot, v, 0), axis=1, keepdims=True)

    def flat(mask, v):
        return jnp.sum(jnp.where(mask, v, 0), axis=0, keepdims=True)

    key = jnp.where(live, key, segments)
    payload = upright(jnp.where(live, payload, 0))
    mine = upright(key)
    before = (key < mine) | ((key == mine) & (lane < slot))
    rank = jnp.sum(before.astype(jnp.int32), axis=1, keepdims=True)
    hit = rank == lane
    keep = (flat(hit, mine) == flat(rank + 1 == lane, mine)) & (lane[:1] > 0)
    upto = flat(mine <= lane, 1)
    have = flat(mine == lane, 1)
    return [flat(hit, slot), flat(hit, payload), keep.astype(jnp.int32), jnp.where(have > 0, upto, 0)]


def kernel(
    counts,
    center,
    halfwidth,
    slot_rows,
    slot_cols,
    blocks_hbm,
    initial,
    out_shifted,
    out_previous,
    meta_vector,
    meta,
    blocks,
    current,
    previous,
    col0,
    col1,
    col2,
    row0,
    row1,
    row2,
    ups,
    lows,
    lsend,
    r1,
    msum,
    msend,
    r2,
    zsend,
    rz,
    usend1,
    ru1,
    usend2,
    ru2,
    load_sem,
    meta_sem,
    initial_sem,
    ssem,
    rsem,
    line_sem,
):
    slots, row_count, col_count = blocks.shape[0], row0.shape[0], col0.shape[0]
    grid_row = lax.axis_index("row")
    grid_col = lax.axis_index("col")
    core = grid_col % 2
    zl = grid_col // 2
    zh = grid_row % HALVES
    x = grid_row // HALVES % RING
    y = grid_row // (HALVES * RING)

    a = x * (1 - core) + y * core
    b = y * (1 - core) + x * core

    def row_of(da=0, db=0, dh=0):
        pa, pb = (a + da) % RING, (b + db) % RING
        px = pa * (1 - core) + pb * core
        py = pb * (1 - core) + pa * core
        return (py * RING + px) * HALVES + (zh + dh) % HALVES

    def place(da=0, db=0, dh=0):
        return (row_of(da, db, dh), grid_col)

    far_end = 3 * (1 - zl // 2)
    near = 1 + zl % 2
    along = (far_end, 6 - zl - far_end - near, near)

    def line(n):
        return (grid_row, along[n] * 2 + core)

    other_core = (grid_row, zl * 2 + 1 - core)

    barrier = pltpu.get_barrier_semaphore()
    peers = [other_core, place(dh=1)]
    peers += [place(da=d) for d in AWAY] + [place(db=d) for d in AWAY]
    peers += [line(n) for n in range(RING - 1)]
    for peer in peers:
        pl.semaphore_signal(barrier, inc=1, device_id=peer, device_id_type=MESH)
    first = pltpu.make_async_copy(initial, current, initial_sem)
    first.start()
    load = pltpu.make_async_copy(blocks_hbm, blocks, load_sem)
    load.start()
    nothing = jnp.zeros(current.shape, F32)
    ups[0] = nothing
    lows[0] = nothing
    live = lax.broadcasted_iota(jnp.int32, (1, slots), 1) < counts[0, 0]
    rows, cols = slot_rows[...], slot_cols[...]
    table = order(rows, cols, live, row_count) + order(cols, rows, live, col_count)
    meta_vector[...] = jnp.zeros_like(meta_vector)
    for n, entry in enumerate(table):
        meta_vector[n : n + 1, 0:slots] = entry
    order_copy = pltpu.make_async_copy(meta_vector, meta, meta_sem)
    order_copy.start()
    first.wait()
    pl.semaphore_wait(barrier, len(peers))

    send_ids, receive_ids = {}, {}

    def copy(leaves, arrives, src, dst, device, by_line=False):
        return pltpu.make_async_remote_copy(
            src_ref=src,
            dst_ref=dst,
            send_sem=ssem.at[send_ids.setdefault(leaves, len(send_ids))],
            recv_sem=line_sem.at[arrives] if by_line else rsem.at[receive_ids.setdefault(arrives, len(receive_ids))],
            device_id=device,
            device_id_type=MESH,
        )

    def wait(arrives, held, by_line=False):
        copy("z", arrives, held, held, other_core, by_line).wait_recv()

    def settle(leaves, held):
        copy(leaves, "z", held, held, other_core).wait_send()

    def settle_last(s):
        settle("mid", msend.at[s])
        settle("up", usend2.at[s])
        settle("back", zsend.at[s])

    def step(s):
        col, row = (col0, col1, col2)[s], (row0, row1, row2)[s]

        def send(leaves, arrives, src, dst, device, by_line=False):
            copy(leaves, arrives, src, dst, device, by_line).start()

        def panel(da=0, db=0, dh=0):
            return col.at[row_of(da, db, dh)]

        def spread1(dh):
            for d in AWAY:
                send("d1", f"d1.{dh}.{d}", panel(dh=dh), panel(dh=dh), place(da=d))

        def spread2(dh, da):
            for d in AWAY:
                held = panel(da=-da, dh=dh)
                send("d2", "d2", held, held, place(db=d))

        def pass2(dh, da):
            wait(f"d1.{dh}.{da}", panel(da=-da, dh=dh))
            spread2(dh, da)

        def row_at(z, which):
            return row.at[z * 2 + which]

        def row_pass(d):
            held = row_at(along[d], core)
            wait(along[d], held, True)
            send("pass", "pass", held, held, other_core)

        def low_end(da, db, dh):
            return meta[L_END, row_of(da, db, dh)]

        def reduce1_start(dh):
            for db in AWAY + (0,):
                for d in AWAY:
                    lsend[s, dh, db, d - 1] = lows[low_end(d, db, dh)].astype(LT)
                    send(
                        "low",
                        f"low.{dh}.{db}",
                        lsend.at[s, dh, db, d - 1],
                        r1.at[s, dh, db, d - 1],
                        place(da=d),
                    )

        def reduce1_end(dh, db):
            total = lows[low_end(0, db, dh)]
            wait(f"low.{dh}.{db}", r1.at[s, dh, db])
            for d in AWAY:
                total = total + r1[s, dh, db, d - 1].astype(F32)
            if db == 0:
                msum[dh] = total
            else:
                msend[s, dh, db - 1] = total.astype(MT)
                send("mid", f"mid.{dh}", msend.at[s, dh, db - 1], r2.at[s, dh, db - 1], place(db=db))

        def reduce2_end(dh):
            total = msum[dh]
            wait(f"mid.{dh}", r2.at[s, dh])
            for d in AWAY:
                total = total + r2[s, dh, d - 1].astype(F32)
            return total

        now = current[...]
        col[row_of()] = now.astype(BF16)
        send("z", "z", panel(), panel(), place(dh=1))
        row[grid_col] = now.T.astype(BF16)
        for d in range(RING - 1):
            send("row", zl, row_at(zl, core), row_at(zl, core), line(d), True)
        send("pass", "pass", row_at(zl, core), row_at(zl, core), other_core)
        spread1(0)
        spread2(0, 0)
        pass2(0, 1)
        pass2(0, 3)
        row_pass(2)
        row_pass(1)
        pass2(0, 2)
        row_pass(0)
        wait("z", panel(dh=1))
        spread1(1)
        spread2(1, 0)
        wait("pass", row.at[0:RING])
        if s:
            settle_last(s - 1)
        if s == 0:
            order_copy.wait()
            load.wait()

        @pl.loop(0, slots // GROUP)
        def _(g):
            total = lows[g * GROUP]
            for i in range(GROUP):
                k = g * GROUP + i
                product = jnp.dot(
                    row[meta[L_PANEL, k]],
                    blocks[meta[L_BLOCK, k]],
                    preferred_element_type=F32,
                )
                total = product + meta[L_KEEP, k].astype(F32) * total
                lows[k + 1] = total

        reduce1_start(1)
        pass2(1, 1)
        pass2(1, 3)
        pass2(1, 2)
        reduce1_start(0)
        for db in AWAY + (0,):
            reduce1_end(1, db)
        wait("d2", col.at[0 : 2 * RING * (RING - 1)])

        @pl.loop(0, slots // GROUP)
        def _(g):
            total = ups[g * GROUP]
            for i in range(GROUP):
                k = g * GROUP + i
                product = jnp.dot(
                    blocks[meta[U_BLOCK, k]],
                    col[meta[U_PANEL, k]],
                    preferred_element_type=F32,
                )
                total = product + meta[U_KEEP, k].astype(F32) * total
                ups[k + 1] = total

        def up_end(z, which):
            return meta[U_END, z * 2 + which]

        for d in range(RING):
            usend1[s, d] = ups[up_end(d, 1 - core)].astype(U1T)
        send("chip", "chip", usend1.at[s], ru1.at[s], other_core)
        zsend[s] = reduce2_end(1).astype(ZT)
        send("back", "back", zsend.at[s], rz.at[s], place(dh=1))
        wait("chip", ru1.at[s])
        for d in range(RING - 1):
            z = along[d]
            usend2[s, d] = (ups[up_end(z, core)] + ru1[s, z].astype(F32)).astype(U2T)
            send("up", "up", usend2.at[s, d], ru2.at[s, zl], line(d))
        upper = ups[up_end(zl, core)] + ru1[s, zl].astype(F32)
        for db in AWAY + (0,):
            reduce1_end(0, db)
        settle("z", panel())
        settle("row", row.at[0 : RING - 1])
        settle("pass", row.at[0:RING])
        settle("d1", col.at[0 : 2 * (RING - 1)])
        settle("d2", col.at[0 : 2 * RING * (RING - 1)])
        settle("low", lsend.at[s])
        settle("chip", usend1.at[s])
        lower = reduce2_end(0)
        wait("up", ru2.at[s, 0 : RING - 1])
        for d in range(RING - 1):
            upper = upper + ru2[s, along[d]].astype(F32)
        wait("back", rz.at[s])
        lower = lower + rz[s].astype(F32)
        applied = upper + lower.T
        shifted = (applied - center[0] * now) / halfwidth[0]
        if s == DEGREE - 1:
            out_shifted[...] = shifted
            out_previous[...] = previous[...]
        else:
            following = shifted if s == 0 else 2.0 * shifted - previous[...]
            previous[...] = now
            current[...] = following

    for s in range(DEGREE):
        step(s)

    settle_last(DEGREE - 1)


def body(hamiltonian_blocks, block_rows, block_cols, block_counts, initial, center, halfwidth):
    stacked = hamiltonian_blocks[0, 0]
    slots, orbitals, _ = stacked.shape
    vectors = initial.shape[1]
    row_count = lax.axis_size("col")
    col_count = lax.axis_size("row")
    steps = DEGREE
    square = (orbitals, vectors)
    vmem = pltpu.VMEM
    scratch = [
        vmem((8, 128), jnp.int32),
        pltpu.SMEM((8, 128), jnp.int32),
        vmem((slots, orbitals, orbitals), BF16),
        vmem(square, F32),
        vmem(square, F32),
        *[vmem((col_count,) + square, BF16)] * steps,
        *[vmem((row_count,) + square, BF16)] * steps,
        vmem((slots + 1,) + square, F32),
        vmem((slots + 1,) + square, F32),
        vmem((steps, 2, RING, RING - 1) + square, LT),
        vmem((steps, 2, RING, RING - 1) + square, LT),
        vmem((2,) + square, F32),
        vmem((steps, 2, RING - 1) + square, MT),
        vmem((steps, 2, RING - 1) + square, MT),
        vmem((steps,) + square, ZT),
        vmem((steps,) + square, ZT),
        vmem((steps, RING) + square, U1T),
        vmem((steps, RING) + square, U1T),
        vmem((steps, RING - 1) + square, U2T),
        vmem((steps, RING) + square, U2T),
        pltpu.SemaphoreType.DMA,
        pltpu.SemaphoreType.DMA,
        pltpu.SemaphoreType.DMA,
        pltpu.SemaphoreType.DMA((10,)),
        pltpu.SemaphoreType.DMA((24,)),
        pltpu.SemaphoreType.DMA((RING,)),
    ]
    smem = pl.BlockSpec(memory_space=pltpu.SMEM)
    whole = pl.BlockSpec(memory_space=pltpu.VMEM)

    hbm = pl.BlockSpec(memory_space=pl.ANY)
    result = jax.ShapeDtypeStruct(square, F32)
    shifted, previous = pl.pallas_call(
        kernel,
        out_shape=(result, result),
        in_specs=[smem, smem, smem, whole, whole, hbm, hbm],
        out_specs=(whole, whole),
        scratch_shapes=scratch,
        compiler_params=pltpu.CompilerParams(collective_id=0, has_side_effects=True),
        name="filter",
    )(block_counts, center, halfwidth, block_rows[0], block_cols[0], stacked, initial)
    return 2.0 * shifted - previous


def solution(mesh):
    in_specs = (
        P("row", "col", None, None, None),
        P("row", "col", None),
        P("row", "col", None),
        P("row", "col"),
        P(("row", "col"), None),
        P(),
        P(),
    )
    out_specs = P(("row", "col"), None)
    return jax.shard_map(body, mesh=mesh, in_specs=in_specs, out_specs=out_specs, check_vma=False)
```

time: 98.5 us -> 89.8 us (0.912)
  Pallas kernels: 89.9 us -> 86.1 us
  local copies, waits for them, and re-layouts: 3.32 us -> 0 us
  other arithmetic: 3.05 us -> 1.51 us
    pallas_call x1, Pallas kernels: 89.9 us -> 86.1 us  [body(): pl.pallas_call(kernel, out_shape=(result, result), in_specs=[smem, smem,...]
    sub x0 -> x1, other arithmetic: none -> 1.51 us  [body(): return 2.0 * shifted - previous]
    unnamed x1 -> x0, local copies, waits for them, and re-layouts: 1.47 us -> none
    convert_element_type x2 -> x0, other arithmetic: 1.44 us -> none  [order(): return [block, panel, keep.astype(jnp.int32), end]]
    slice x2 -> x0, local copies, waits for them, and re-layouts: 1.18 us -> none  [order(): keep = (sorted_key == jnp.roll(sorted_key, 1)) & (slot > 0)]
where the time goes in v3:
time: 89.8 us; the launch traced here: 89.6 us
  Pallas kernels  86.1 us (96%)
  between operations  1.95 us (2%)
  other arithmetic  1.51 us (2%)
    pallas_call x1, Pallas kernels, body(): pl.pallas_call(kernel, out_shape=(result, result), in_specs=[smem, smem,...  86.1 us

profile of v3, /device:TPU:1, one launch (start us, length us, event | category | flops | bytes accessed | tf_op | source)
XLA Modules:
  0.0 89.6 jit_solution(5744635543163871586)
XLA Ops:
  1.9 86.1 %filter.1 = (f32[128,128]{1,0:T(8,128)}, f32[128,128]{1,0:T(8,128)}) custom-call(s32[1,1]{1,0:T(1,128)S(6)} %copy.8.counts, f32[1]{0:T(128)S(6)} %copy.9.center, f32[1]{0:T(128)S(6)} %copy.10.halfwidth, s32[1,64]{1,0:T(1,128)} %bitcast.4, s32[1,64]{1,0:T(1,128)} %bitcast.5, bf16[64,128,128]{2,1,0:T(8,128)(2,1)} %bitcast.3, f32[128,128]{1,0:T(8,128)} %initial.1), custom_call_target="tpu_custom_call" | custom-call | tf_op jit(solution)/shard_map/filter/pallas_call | solution.py:379
  88.1 1.5 %multiply_subtract_fusion = f32[128,128]{1,0:T(8,128)} fusion(f32[128,128]{1,0:T(8,128)} %get-tuple-element.8, f32[128,128]{1,0:T(8,128)} %get-tuple-element.7), kind=kLoop, calls=%fused_computation | loop fusion | flops 32768 | bytes 196608 | tf_op jit(solution)/shard_map/sub | solution.py:388

commit v4 on v3

--- a/solution.py
+++ b/solution.py
@@ -182,7 +182,7 @@
         def spread2(dh, da):
             for d in AWAY:
                 held = panel(da=-da, dh=dh)
-                send("d2", "d2", held, held, place(db=d))
+                send("d2", f"d2.{s}" if da or dh else "d2own", held, held, place(db=d))
 
         def pass2(dh, da):
             wait(f"d1.{dh}.{da}", panel(da=-da, dh=dh))
@@ -200,27 +200,27 @@
             return meta[L_END, row_of(da, db, dh)]
 
         def reduce1_start(dh):
-            for db in AWAY + (0,):
+            for da in AWAY + (0,):
                 for d in AWAY:
-                    lsend[s, dh, db, d - 1] = lows[low_end(d, db, dh)].astype(LT)
+                    lsend[s, dh, da, d - 1] = lows[low_end(da, d, dh)].astype(LT)
                     send(
                         "low",
-                        f"low.{dh}.{db}",
-                        lsend.at[s, dh, db, d - 1],
-                        r1.at[s, dh, db, d - 1],
-                        place(da=d),
+                        f"low.{dh}.{da}",
+                        lsend.at[s, dh, da, d - 1],
+                        r1.at[s, dh, da, d - 1],
+                        place(db=d),
                     )
 
-        def reduce1_end(dh, db):
-            total = lows[low_end(0, db, dh)]
-            wait(f"low.{dh}.{db}", r1.at[s, dh, db])
+        def reduce1_end(dh, da):
+            total = lows[low_end(da, 0, dh)]
+            wait(f"low.{dh}.{da}", r1.at[s, dh, da])
             for d in AWAY:
-                total = total + r1[s, dh, db, d - 1].astype(F32)
-            if db == 0:
+                total = total + r1[s, dh, da, d - 1].astype(F32)
+            if da == 0:
                 msum[dh] = total
             else:
-                msend[s, dh, db - 1] = total.astype(MT)
-                send("mid", f"mid.{dh}", msend.at[s, dh, db - 1], r2.at[s, dh, db - 1], place(db=db))
+                msend[s, dh, da - 1] = total.astype(MT)
+                send("mid", f"mid.{dh}", msend.at[s, dh, da - 1], r2.at[s, dh, da - 1], place(da=da))
 
         def reduce2_end(dh):
             total = msum[dh]
@@ -247,6 +247,7 @@
         wait("z", panel(dh=1))
         spread1(1)
         spread2(1, 0)
+        wait("d2own", col.at[0 : RING - 1])
         wait("pass", row.at[0:RING])
         if s:
             settle_last(s - 1)
@@ -274,7 +275,7 @@
         reduce1_start(0)
         for db in AWAY + (0,):
             reduce1_end(1, db)
-        wait("d2", col.at[0 : 2 * RING * (RING - 1)])
+        wait(f"d2.{s}", col.at[0 : (2 * RING - 1) * (RING - 1)])
 
         @pl.loop(0, slots // GROUP)
         def _(g):
@@ -368,7 +369,7 @@
         pltpu.SemaphoreType.DMA,
         pltpu.SemaphoreType.DMA,
         pltpu.SemaphoreType.DMA((10,)),
-        pltpu.SemaphoreType.DMA((24,)),
+        pltpu.SemaphoreType.DMA((27,)),
         pltpu.SemaphoreType.DMA((RING,)),
     ]
     smem = pl.BlockSpec(memory_space=pltpu.SMEM)

time: 89.8 us -> 87.6 us (0.976)
  Pallas kernels: 86.1 us -> 84 us
    pallas_call x1, Pallas kernels: 86.1 us -> 84 us  [body(): pl.pallas_call(kernel, out_shape=(result, result), in_specs=[smem, smem,...]
where the time goes in v4:
time: 87.6 us; the launch traced here: 87.4 us
  Pallas kernels  84 us (96%)
  between operations  1.95 us (2%)
  other arithmetic  1.51 us (2%)
    pallas_call x1, Pallas kernels, body(): pl.pallas_call(kernel, out_shape=(result, result), in_specs=[smem, smem,...  84 us

profile of v4, /device:TPU:1, one launch (start us, length us, event | category | flops | bytes accessed | tf_op | source)
XLA Modules:
  0.0 87.4 jit_solution(5564174627895228093)
XLA Ops:
  1.9 84.0 %filter.1 = (f32[128,128]{1,0:T(8,128)}, f32[128,128]{1,0:T(8,128)}) custom-call(s32[1,1]{1,0:T(1,128)S(6)} %copy.8.counts, f32[1]{0:T(128)S(6)} %copy.9.center, f32[1]{0:T(128)S(6)} %copy.10.halfwidth, s32[1,64]{1,0:T(1,128)} %bitcast.4, s32[1,64]{1,0:T(1,128)} %bitcast.5, bf16[64,128,128]{2,1,0:T(8,128)(2,1)} %bitcast.3, f32[128,128]{1,0:T(8,128)} %initial.1), custom_call_target="tpu_custom_call" | custom-call | tf_op jit(solution)/shard_map/filter/pallas_call | solution.py:380
  85.9 1.5 %multiply_subtract_fusion = f32[128,128]{1,0:T(8,128)} fusion(f32[128,128]{1,0:T(8,128)} %get-tuple-element.8, f32[128,128]{1,0:T(8,128)} %get-tuple-element.7), kind=kLoop, calls=%fused_computation | loop fusion | flops 32768 | bytes 196608 | tf_op jit(solution)/shard_map/sub | solution.py:389

commit v5 on v4

--- a/solution.py
+++ b/solution.py
@@ -293,16 +293,17 @@
         def up_end(z, which):
             return meta[U_END, z * 2 + which]
 
-        for d in range(RING):
-            usend1[s, d] = ups[up_end(d, 1 - core)].astype(U1T)
-        send("chip", "chip", usend1.at[s], ru1.at[s], other_core)
+        for n, z in enumerate(along + (zl,)):
+            usend1[s, z] = ups[up_end(z, 1 - core)].astype(U1T)
+            send("chip", f"chip.{n}", usend1.at[s, z], ru1.at[s, z], other_core)
         zsend[s] = reduce2_end(1).astype(ZT)
         send("back", "back", zsend.at[s], rz.at[s], place(dh=1))
-        wait("chip", ru1.at[s])
         for d in range(RING - 1):
             z = along[d]
+            wait(f"chip.{d}", ru1.at[s, z])
             usend2[s, d] = (ups[up_end(z, core)] + ru1[s, z].astype(F32)).astype(U2T)
             send("up", "up", usend2.at[s, d], ru2.at[s, zl], line(d))
+        wait(f"chip.{RING - 1}", ru1.at[s, zl])
         upper = ups[up_end(zl, core)] + ru1[s, zl].astype(F32)
         for db in AWAY + (0,):
             reduce1_end(0, db)
@@ -369,7 +370,7 @@
         pltpu.SemaphoreType.DMA,
         pltpu.SemaphoreType.DMA,
         pltpu.SemaphoreType.DMA((10,)),
-        pltpu.SemaphoreType.DMA((27,)),
+        pltpu.SemaphoreType.DMA((30,)),
         pltpu.SemaphoreType.DMA((RING,)),
     ]
     smem = pl.BlockSpec(memory_space=pltpu.SMEM)

time: 87.6 us -> 87.7 us (level)
  no operation moved by 1% of the time
where the time goes in v5:
time: 87.7 us; the launch traced here: 87.5 us
  Pallas kernels  84.1 us (96%)
  between operations  1.95 us (2%)
  other arithmetic  1.51 us (2%)
    pallas_call x1, Pallas kernels, body(): pl.pallas_call(kernel, out_shape=(result, result), in_specs=[smem, smem,...  84.1 us

profile of v5, /device:TPU:1, one launch (start us, length us, event | category | flops | bytes accessed | tf_op | source)
XLA Modules:
  0.0 87.5 jit_solution(9129032407581136545)
XLA Ops:
  1.9 84.1 %filter.1 = (f32[128,128]{1,0:T(8,128)}, f32[128,128]{1,0:T(8,128)}) custom-call(s32[1,1]{1,0:T(1,128)S(6)} %copy.8.counts, f32[1]{0:T(128)S(6)} %copy.9.center, f32[1]{0:T(128)S(6)} %copy.10.halfwidth, s32[1,64]{1,0:T(1,128)} %bitcast.4, s32[1,64]{1,0:T(1,128)} %bitcast.5, bf16[64,128,128]{2,1,0:T(8,128)(2,1)} %bitcast.3, f32[128,128]{1,0:T(8,128)} %initial.1), custom_call_target="tpu_custom_call" | custom-call | tf_op jit(solution)/shard_map/filter/pallas_call | solution.py:381
  86.0 1.5 %multiply_subtract_fusion = f32[128,128]{1,0:T(8,128)} fusion(f32[128,128]{1,0:T(8,128)} %get-tuple-element.8, f32[128,128]{1,0:T(8,128)} %get-tuple-element.7), kind=kLoop, calls=%fused_computation | loop fusion | flops 32768 | bytes 196608 | tf_op jit(solution)/shard_map/sub | solution.py:390
